TPU v7x, 32 devices: a whole 2x2x4 slice. The times are simulated.
32 devices in a mesh: dp: 8 (over y, x, core), tensor: 4 (over z).
Axes of the slice: x: 2, y: 2, z: 4, core: 2. Of those that a mesh axis runs over, the one named last changes fastest.
Arguments:
- images: bfloat16 [64, 257, 1664], P(('dp', 'tensor')), may hold values from -6 to 6
- first_gain: float32 [1664], replicated, may hold values from 0.5 to 1.5
- first_shift: float32 [1664], replicated, may hold values from -4 to 4
- qkv_weight: bfloat16 [3, 1664, 1664], P(None, None, 'tensor'), as said below
- qv_bias: float32 [2, 1664], P(None, 'tensor'), may hold values from -6 to 6
- out_weight: bfloat16 [1664, 1664], P('tensor'), may hold values from -0.625 to 0.625
- out_bias: float32 [1664], replicated, may hold values from -4 to 4
- second_gain: float32 [1664], replicated, may hold values from 0.5 to 1.5
- second_shift: float32 [1664], replicated, may hold values from -4 to 4
- up_weight: bfloat16 [1664, 8192], P(None, 'tensor'), may hold values from -0.15625 to 0.15625
- up_bias: float32 [8192], P('tensor'), may hold values from -6 to 6
- down_weight: bfloat16 [8192, 1664], P('tensor'), may hold values from -0.0625 to 0.0625
- down_bias: float32 [1664], replicated, may hold values from -4 to 4
- cotangent: bfloat16 [64, 257, 1664], P(('dp', 'tensor')), may hold values from -6 to 6
Outputs:
- result: bfloat16 [64, 257, 1664], P(('dp', 'tensor'))
- grad_images: bfloat16 [64, 257, 1664], P(('dp', 'tensor'))
- grad_first_gain: float32 [1664], replicated
- grad_first_shift: float32 [1664], replicated
- grad_qkv_weight: float32 [3, 1664, 1664], P(None, None, 'tensor')
- grad_qv_bias: float32 [2, 1664], P(None, 'tensor')
- grad_out_weight: float32 [1664, 1664], P('tensor')
- grad_out_bias: float32 [1664], replicated
- grad_second_gain: float32 [1664], replicated
- grad_second_shift: float32 [1664], replicated
- grad_up_weight: float32 [1664, 8192], P(None, 'tensor')
- grad_up_bias: float32 [8192], P('tensor')
- grad_down_weight: float32 [8192, 1664], P('tensor')
- grad_down_bias: float32 [1664], replicated
Inputs may be any that keep to these rules, and one draw needn't show every extreme that they name: `qkv_weight`: the three parts are query, keys and values, in this order.
All inputs are finite; a program needn't handle non-finite values.
Results may differ from a plain program's by a relative error of at most 0.02.
Values may be sent and summed in bfloat16 or wider, within the bound.
A program may use at most 256 MiB of HBM per device.

v0:
```python
import jax
import jax.numpy as jnp
from jax import lax
from jax.sharding import PartitionSpec as P

HD = 104
epsilon = 1e-06
inv_root_two = 0.7071067811865476
inv_root_tau = 0.3989422804014327


def normalize(rows):
    centre = jnp.mean(rows, axis=-1, keepdims=True)
    centred = rows - centre
    spread = jnp.mean(centred * centred, axis=-1, keepdims=True)
    inverse = lax.rsqrt(spread + epsilon)
    return (centred * inverse, inverse)


def norm_back(grad, unit, inverse, gain):
    scaled = grad * gain
    first = jnp.mean(scaled, axis=-1, keepdims=True)
    second = jnp.mean(scaled * unit, axis=-1, keepdims=True)
    return inverse * (scaled - first - unit * second)


def attend_block(query, keys, values):
    factor = query.shape[-1] ** (-0.5)
    scores = jnp.einsum("bshd,bthd->bhst", query, keys, preferred_element_type=jnp.float32) * factor
    top = jnp.max(scores, axis=-1, keepdims=True)
    raised = jnp.exp(scores - top)
    total = jnp.sum(raised, axis=-1, keepdims=True)
    weights = (raised / total).astype(jnp.bfloat16)
    mixed = jnp.einsum("bhst,bthd->bshd", weights, values, preferred_element_type=jnp.float32)
    return (mixed, (top + jnp.log(total))[..., 0])


def attend_back(query, keys, values, grad_out, log_total):
    factor = query.shape[-1] ** (-0.5)
    scores = jnp.einsum("bshd,bthd->bhst", query, keys, preferred_element_type=jnp.float32) * factor
    probs = jnp.exp(scores - log_total[..., None])
    grad_values = jnp.einsum(
        "bhst,bshd->bthd", probs.astype(jnp.bfloat16), grad_out, preferred_element_type=jnp.float32
    )
    grad_probs = jnp.einsum("bshd,bthd->bhst", grad_out, values, preferred_element_type=jnp.float32)
    inner = jnp.sum(probs * grad_probs, axis=-1, keepdims=True)
    grad_scores = (probs * (grad_probs - inner)).astype(jnp.bfloat16)
    grad_query = (
        jnp.einsum("bhst,bthd->bshd", grad_scores, keys, preferred_element_type=jnp.float32)
        * factor
    )
    grad_keys = (
        jnp.einsum("bhst,bshd->bthd", grad_scores, query, preferred_element_type=jnp.float32)
        * factor
    )
    return (
        grad_query.astype(jnp.bfloat16),
        grad_keys.astype(jnp.bfloat16),
        grad_values.astype(jnp.bfloat16),
    )


def on_device(
    images,
    first_gain,
    first_shift,
    qkv_weight,
    qv_bias,
    out_weight,
    out_bias,
    second_gain,
    second_shift,
    up_weight,
    up_bias,
    down_weight,
    down_bias,
    cotangent,
):
    seq_len = images.shape[1]
    columns = qkv_weight.shape[2]
    heads_here = columns // HD
    inputs = images.astype(jnp.float32)
    unit_first, inverse_first = normalize(inputs)
    normed_local = (unit_first * first_gain + first_shift).astype(jnp.bfloat16)
    normed_first = lax.all_gather(normed_local, "tensor", axis=0, tiled=True)
    count = normed_first.shape[0]
    projected = jnp.einsum(
        "isd,nde->nise", normed_first, qkv_weight, preferred_element_type=jnp.float32
    )
    query = (projected[0] + qv_bias[0]).astype(jnp.bfloat16)
    keys = projected[1].astype(jnp.bfloat16)
    values = (projected[2] + qv_bias[1]).astype(jnp.bfloat16)
    split = (count // 2, 2, seq_len, heads_here, HD)
    query_blocks = query.reshape(split)
    key_blocks = keys.reshape(split)
    value_blocks = values.reshape(split)
    mixed, log_total = lax.map(
        lambda triple: attend_block(triple[0], triple[1], triple[2]),
        (query_blocks, key_blocks, value_blocks),
    )
    heads_out = mixed.reshape(count, seq_len, columns).astype(jnp.bfloat16)
    piece = heads_out
    attention = lax.psum_scatter(
        jnp.einsum("isc,cd->isd", piece, out_weight, preferred_element_type=jnp.float32).astype(
            jnp.bfloat16
        ),
        "tensor",
        scatter_dimension=0,
        tiled=True,
    ).astype(jnp.float32)
    middle = inputs + (attention + out_bias)
    unit_second, inverse_second = normalize(middle)
    normed_second = lax.all_gather(
        (unit_second * second_gain + second_shift).astype(jnp.bfloat16),
        "tensor",
        axis=0,
        tiled=True,
    )
    hidden = (
        jnp.einsum("isd,df->isf", normed_second, up_weight, preferred_element_type=jnp.float32)
        + up_bias
    )
    active = jax.nn.gelu(hidden, approximate=False).astype(jnp.bfloat16)
    piece = active
    result = (
        middle
        + lax.psum_scatter(
            jnp.einsum(
                "isf,fd->isd", piece, down_weight, preferred_element_type=jnp.float32
            ).astype(jnp.bfloat16),
            "tensor",
            scatter_dimension=0,
            tiled=True,
        ).astype(jnp.float32)
        + down_bias
    ).astype(jnp.bfloat16)
    seed_rows = lax.all_gather(cotangent, "tensor", axis=0, tiled=True)
    grad_down_weight = jnp.einsum(
        "isf,isd->fd", active, seed_rows, preferred_element_type=jnp.float32
    )
    grad_down_bias = jnp.sum(cotangent, axis=(0, 1), dtype=jnp.float32)
    grad_active = jnp.einsum(
        "isd,fd->isf", seed_rows, down_weight, preferred_element_type=jnp.float32
    )
    normal_cdf = 0.5 * (1.0 + lax.erf(hidden * inv_root_two))
    density = jnp.exp(-0.5 * hidden * hidden) * inv_root_tau
    grad_hidden = (grad_active * (normal_cdf + hidden * density)).astype(jnp.bfloat16)
    grad_up_weight = jnp.einsum(
        "isd,isf->df", normed_second, grad_hidden, preferred_element_type=jnp.float32
    )
    grad_up_bias = jnp.sum(grad_hidden, axis=(0, 1), dtype=jnp.float32)
    piece = grad_hidden
    grad_normed_second = lax.psum_scatter(
        jnp.einsum("isf,df->isd", piece, up_weight, preferred_element_type=jnp.float32).astype(
            jnp.bfloat16
        ),
        "tensor",
        scatter_dimension=0,
        tiled=True,
    ).astype(jnp.float32)
    grad_second_gain = jnp.sum(grad_normed_second * unit_second, axis=(0, 1))
    grad_second_shift = jnp.sum(grad_normed_second, axis=(0, 1))
    grad_middle = cotangent.astype(jnp.float32) + norm_back(
        grad_normed_second, unit_second, inverse_second, second_gain
    )
    grad_branch = grad_middle.astype(jnp.bfloat16)
    grad_out_bias = jnp.sum(grad_branch, axis=(0, 1), dtype=jnp.float32)
    branch_rows = lax.all_gather(grad_branch, "tensor", axis=0, tiled=True)
    grad_out_weight = jnp.einsum(
        "isc,isd->cd", heads_out, branch_rows, preferred_element_type=jnp.float32
    )
    grad_heads = jnp.einsum(
        "isd,cd->isc", branch_rows, out_weight, preferred_element_type=jnp.float32
    ).astype(jnp.bfloat16)
    grad_query, grad_keys, grad_values = lax.map(
        lambda parts: attend_back(parts[0], parts[1], parts[2], parts[3], parts[4]),
        (query_blocks, key_blocks, value_blocks, grad_heads.reshape(split), log_total),
    )
    grad_projected = jnp.stack(
        [
            grad_query.reshape(count, seq_len, columns),
            grad_keys.reshape(count, seq_len, columns),
            grad_values.reshape(count, seq_len, columns),
        ]
    )
    grad_qkv_weight = jnp.einsum(
        "isd,nisc->ndc", normed_first, grad_projected, preferred_element_type=jnp.float32
    )
    grad_qv_bias = jnp.stack(
        [
            jnp.sum(grad_projected[0], axis=(0, 1), dtype=jnp.float32),
            jnp.sum(grad_projected[2], axis=(0, 1), dtype=jnp.float32),
        ]
    )
    piece = grad_projected
    grad_normed_first = lax.psum_scatter(
        jnp.einsum("nisc,ndc->isd", piece, qkv_weight, preferred_element_type=jnp.float32).astype(
            jnp.bfloat16
        ),
        "tensor",
        scatter_dimension=0,
        tiled=True,
    ).astype(jnp.float32)
    grad_first_gain = jnp.sum(grad_normed_first * unit_first, axis=(0, 1))
    grad_first_shift = jnp.sum(grad_normed_first, axis=(0, 1))
    grad_images = (
        grad_middle + norm_back(grad_normed_first, unit_first, inverse_first, first_gain)
    ).astype(jnp.bfloat16)
    (
        grad_qkv_weight,
        grad_qv_bias,
        grad_out_weight,
        grad_up_weight,
        grad_up_bias,
        grad_down_weight,
    ) = (
        lax.psum(grad_qkv_weight.astype(jnp.bfloat16), "dp").astype(jnp.float32),
        lax.psum(grad_qv_bias.astype(jnp.bfloat16), "dp").astype(jnp.float32),
        lax.psum(grad_out_weight.astype(jnp.bfloat16), "dp").astype(jnp.float32),
        lax.psum(grad_up_weight.astype(jnp.bfloat16), "dp").astype(jnp.float32),
        lax.psum(grad_up_bias.astype(jnp.bfloat16), "dp").astype(jnp.float32),
        lax.psum(grad_down_weight.astype(jnp.bfloat16), "dp").astype(jnp.float32),
    )
    (
        grad_first_gain,
        grad_first_shift,
        grad_out_bias,
        grad_second_gain,
        grad_second_shift,
        grad_down_bias,
    ) = lax.psum(
        (
            grad_first_gain,
            grad_first_shift,
            grad_out_bias,
            grad_second_gain,
            grad_second_shift,
            grad_down_bias,
        ),
        ("dp", "tensor"),
    )
    return (
        result,
        grad_images,
        grad_first_gain,
        grad_first_shift,
        grad_qkv_weight,
        grad_qv_bias,
        grad_out_weight,
        grad_out_bias,
        grad_second_gain,
        grad_second_shift,
        grad_up_weight,
        grad_up_bias,
        grad_down_weight,
        grad_down_bias,
    )


def solution(mesh):
    return jax.shard_map(
        on_device,
        mesh=mesh,
        in_specs=(
            P(("dp", "tensor"), None, None),
            P(),
            P(),
            P(None, None, "tensor"),
            P(None, "tensor"),
            P("tensor", None),
            P(),
            P(),
            P(),
            P(None, "tensor"),
            P("tensor"),
            P("tensor", None),
            P(),
            P(("dp", "tensor"), None, None),
        ),
        out_specs=(
            P(("dp", "tensor"), None, None),
            P(("dp", "tensor"), None, None),
            P(),
            P(),
            P(None, None, "tensor"),
            P(None, "tensor"),
            P("tensor", None),
            P(),
            P(),
            P(),
            P(None, "tensor"),
            P("tensor"),
            P("tensor", None),
            P(),
        ),
        check_vma=False,
    )
```

profile of v0, /device:TPU:0, one launch (start us, length us, event | category | flops | bytes accessed | tf_op | source)
XLA Modules:
  0.0 1597.7 jit_solution(3615522905375342727)
XLA Ops:
  14.7 130.0 %all-gather.5.cloned.1.call-done = bf16[8,257,1664]{2,1,0:T(8,128)(2,1)} async-done(((bf16[2,257,1664]{2,1,0:T(8,128)(2,1)}), bf16[8,257,1664]{2,1,0:T(8,128)(2,1)}) %all-gather.5.cloned.1.call-update) | async-done | bytes 6842384 | tf_op jit(solution)/shard_map/all_gather | solution.py:85
  144.7 15.5 convolution_bitcast_fusion
  166.4 5.9 reshape.134
  177.4 5.9 reshape.135
  196.2 24.4 %while.26 = (s32[]{:T(128)}, bf16[4,2,257,4,104]{4,2,3,1,0:T(8,128)(2,1)}, f32[4,2,4,257]{3,2,1,0:T(4,128)}, bf16[4,2,257,4,104]{4,2,3,1,0:T(8,128)(2,1)}, bf16[...) while((s32[]{:T(128)}, bf16[4,2,257,4,104]{4,2,3,1,0:T(8,128)(2,1)}, ...), condition=%wide.region_5.6_spmd, body=%wide.region_2.5_spmd.sunk | while | flops 224564544 | bytes 9116557 | solution.py:97
  228.9 8.1 convolution_convert_fusion
  237.2 121.2 %reduce-scatter.5.cloned.1.call-done = bf16[2,257,1664]{2,1,0:T(8,128)(2,1)} async-done(((bf16[8,257,1664]{2,1,0:T(8,128)(2,1)}), bf16[2,257,1664]{2,1,0:T(8,128)(2,1)}) %reduce-scatter.5.cloned.1.call-update) | async-done | bytes 1710608 | tf_op jit(solution)/shard_map/reduce_scatter | solution.py:103
  366.6 125.1 %all-gather.7.cloned.1.call-done = bf16[8,257,1664]{2,1,0:T(8,128)(2,1)} async-done(((bf16[2,257,1664]{2,1,0:T(8,128)(2,1)}), bf16[8,257,1664]{2,1,0:T(8,128)(2,1)}) %all-gather.7.cloned.1.call-update) | async-done | bytes 6842384 | tf_op jit(solution)/shard_map/all_gather | solution.py:113
  491.7 28.5 %fusion.91 = (u8[257,2048]{1,0:T(8,128)(4,1)}, u8[257,2048]{1,0:T(8,128)(4,1)}, f32[8,257,2048]{2,1,0:T(8,128)}) fusion(f32[2048]{0:T(1024)S(1)} %copy-done.39, bf16[8,257,1664]{2,1,0:T(8,128)(2,1)} %all-gather.7.cloned.1.call-done, bf16[1664,2048]{1,0:T(8,128)(2,1)} %param.27), kind=kOutput, calls=%fused_computation.123 | convolution fusion | flops 14071066624 | bytes 31561728 | tf_op jit(solution)/shard_map/isd,df->isf/dot_general | solution.py:120
  520.2 99.3 %all-gather.9.cloned.1.call-done = bf16[8,257,1664]{2,1,0:T(8,128)(2,1)} async-done(((bf16[2,257,1664]{2,1,0:T(8,128)(2,1)}), bf16[8,257,1664]{2,1,0:T(8,128)(2,1)}) %all-gather.9.cloned.1.call-update) | async-done | bytes 6842384 | tf_op jit(solution)/shard_map/all_gather | solution.py:137
  619.5 29.1 %fusion.123 = (bf16[2048]{0:T(1024)(128)(2,1)}, bf16[8,257,2048]{2,1,0:T(8,128)(2,1)S(1)}) fusion(f32[8,257,2048]{2,1,0:T(8,128)} %get-tuple-element.253, f32[2048]{0:T(1024)S(1)} %copy-done.39, bf16[8,257,1664]{2,1,0:T(8,128)(2,1)} %all-gather.9.cloned.1.call-done, bf16[2048,1664]{1,0:T(8,128)(2,1)} %param.29), kind=kOutput, calls=%fused_computation.175 | convolution fusion | flops 14063695872 | bytes 38934528 | tf_op jit(solution)/shard_map/isd,fd->isf/dot_general | solution.py:142
  652.1 21.0 %fusion.78 = bf16[8,257,1664]{2,1,0:T(8,128)(2,1)} fusion(bf16[8,257,2048]{2,1,0:T(8,128)(2,1)S(1)} %get-tuple-element.255, bf16[1664,2048]{1,0:T(8,128)(2,1)} %param.27), kind=kOutput, calls=%fused_computation.102 | convolution fusion | flops 14016590848 | bytes 22079488 | tf_op jit(solution)/shard_map/isf,df->isd/dot_general | solution.py:154
  673.2 121.2 %reduce-scatter.9.cloned.1.call-done = bf16[2,257,1664]{2,1,0:T(8,128)(2,1)} async-done(((bf16[8,257,1664]{2,1,0:T(8,128)(2,1)}), bf16[2,257,1664]{2,1,0:T(8,128)(2,1)}) %reduce-scatter.9.cloned.1.call-update) | async-done | bytes 1710608 | tf_op jit(solution)/shard_map/reduce_scatter | solution.py:153
  802.8 42.3 %fusion.52 = bf16[8,257,2048]{2,1,0:T(8,128)(2,1)S(1)} fusion(f32[8,257,2048]{2,1,0:T(8,128)} %get-tuple-element.253, f32[2048]{0:T(1024)S(1)} %copy-done.39, u8[257,2048]{1,0:T(8,128)(4,1)} %get-tuple-element.189, u8[257,2048]{1,0:T(8,128)(4,1)} %get-tuple-element.188), kind=kLoop, calls=%fused_computation.60 | loop fusion | flops 298958848 | bytes 26324992 | tf_op jit(solution)/shard_map/convert_element_type | solution.py:123
  845.2 25.8 %bitcast_convert_fusion.1 = bf16[2048,1664]{1,0:T(8,128)(2,1)} fusion(bf16[8,257,2048]{2,1,0:T(8,128)(2,1)S(1)} %fusion.52, bf16[8,257,1664]{2,1,0:T(8,128)(2,1)} %all-gather.9.cloned.1.call-done), kind=kOutput, calls=%fused_computation.86 | convolution fusion | flops 14016577536 | bytes 22079488 | tf_op jit(solution)/shard_map/isf,isd->fd/dot_general | solution.py:138
  871.1 18.5 %bitcast_convert_fusion.2 = bf16[1664,2048]{1,0:T(8,128)(2,1)} fusion(bf16[8,257,1664]{2,1,0:T(8,128)(2,1)S(1)} %bitcast.177, bf16[8,257,2048]{2,1,0:T(8,128)(2,1)S(1)} %bitcast.179), kind=kOutput, calls=%fused_computation.87 | convolution fusion | flops 14016577536 | bytes 22079488 | tf_op jit(solution)/shard_map/isd,isf->df/dot_general | solution.py:148
  889.5 41.3 %all-gather.11.cloned.1.call-done = bf16[8,257,1664]{2,1,0:T(8,128)(2,1)} async-done(((bf16[2,257,1664]{2,1,0:T(8,128)(2,1)}), bf16[8,257,1664]{2,1,0:T(8,128)(2,1)}) %all-gather.11.cloned.1.call-update) | async-done | bytes 6842384 | tf_op jit(solution)/shard_map/all_gather | solution.py:168
  930.8 8.4 convolution_convert_fusion.1
  939.3 4.9 reshape.137
  944.1 50.2 %while.27 = (s32[]{:T(128)}, bf16[4,2,257,4,104]{4,2,3,1,0:T(8,128)(2,1)}, bf16[4,2,257,4,104]{4,3,2,1,0:T(4,128)(2,1)}, bf16[4,2,257,4,104]{4,2,3,1,0:T(8,128)(...) while((s32[]{:T(128)}, ...), condition=%wide.region_15.16_spmd, body=%wide.region_13.15_spmd.sunk | while | flops 556935424 | bytes 23355692 | solution.py:175
  1018.3 8.0 fusion.116
  1026.3 15.7 fusion.98
  1042.1 15.3 bitcast_convert_fusion
  1057.5 21.5 %fusion.81 = bf16[8,257,1664]{2,1,0:T(8,128)(2,1)} fusion(bf16[8,257,2048]{2,1,0:T(8,128)(2,1)} %copy-done.9, bf16[2048,1664]{1,0:T(8,128)(2,1)} %param.29), kind=kOutput, calls=%fused_computation.103 | convolution fusion | flops 14016590848 | bytes 22079488 | tf_op jit(solution)/shard_map/isf,fd->isd/dot_general | solution.py:128
  1083.3 15.5 all-reduce.1
  1100.1 186.1 %all-reduce.5.cloned.1.call-done = (bf16[3,1664,416]{1,2,0:T(8,128)(2,1)}, bf16[416,1664]{1,0:T(8,128)(2,1)}, bf16[1664,2048]{1,0:T(8,128)(2,1)}, bf16[2048,1664]{1,0:T(8,128)(2,1)}) async-done(((bf16[3,1664,416]{1,2,0:T(8,128)(2,1)}, bf16[416,1664]{1,0:T(8,128)(2,1)}, bf16[1664,2048]{1,0:T(8,128)(2,1)}, bf16[2048,1664]{1,0:T(8,128)(2,1)}), (bf16[3,1664,416]{1,2,0:T(8,128)(2,1)}, ...) | async-done | bytes 19169296 | tf_op jit(solution)/shard_map/psum | solution.py:217
  1286.1 10.6 convert_element_type.181
  1296.7 6.0 convert_element_type.184
  1308.4 102.9 %reduce-scatter.11.cloned.1.call-done = bf16[2,257,1664]{2,1,0:T(8,128)(2,1)} async-done(((bf16[8,257,1664]{2,1,0:T(8,128)(2,1)}), bf16[2,257,1664]{2,1,0:T(8,128)(2,1)}) %reduce-scatter.11.cloned.1.call-update) | async-done | bytes 1710608 | tf_op jit(solution)/shard_map/reduce_scatter | solution.py:196
  1414.4 122.8 %reduce-scatter.7.cloned.1.call-done = bf16[2,257,1664]{2,1,0:T(8,128)(2,1)} async-done(((bf16[8,257,1664]{2,1,0:T(8,128)(2,1)}), bf16[2,257,1664]{2,1,0:T(8,128)(2,1)}) %reduce-scatter.7.cloned.1.call-update) | async-done | bytes 1710608 | tf_op jit(solution)/shard_map/reduce_scatter | solution.py:127
  1537.3 6.5 fusion.108
  1548.9 42.1 %all-reduce = (f32[1664]{0:T(1024)}, f32[1664]{0:T(1024)}, f32[1664]{0:T(1024)}, f32[1664]{0:T(1024)}, f32[1664]{0:T(1024)}, /*index=5*/f32[1664]{0:T(1024)}) all-reduce(f32[1664]{0:T(1024)S(1)} %get-tuple-element.192, f32[1664]{0:T(1024)S(1)} %get-tuple-element.197, ...), channel_id=1, replica_groups=mesh['dp'=8,'tensor'=4] {'dp','tensor'}, use_global_device_ids=true, to_apply=%region_20.21 | all-reduce | flops 9984 | bytes 79872 | tf_op jit(solution)/shard_map/psum | solution.py:231
  (224 shorter events, 177.9 us)
Async XLA Ops:
  7.2 221.7 %copy-start = (bf16[416,1664]{1,0:T(8,128)(2,1)S(1)}, bf16[416,1664]{1,0:T(8,128)(2,1)}, u32[]{:S(2)}) copy-start(bf16[416,1664]{1,0:T(8,128)(2,1)} %param.23) | copy-start | bytes 4153348
  7.2 137.5 %all-gather.5.cloned.1.call-start = ((), (), s32[]{:S(2)}) async-start(), calls=%async_computation.4 | async-start | bytes 8785920 | tf_op jit(solution)/shard_map/all_gather | solution.py:85
  14.5 343.9 %reduce-scatter.5.cloned.1.call-start = ((), (), s32[]{:S(2)}) async-start(), calls=%async_computation.5 | async-start | bytes 8785920 | tf_op jit(solution)/shard_map/reduce_scatter | solution.py:103
  237.1 121.3 %copy-start.17 = (f32[1664]{0:T(1024)S(1)}, f32[1664]{0:T(1024)}, u32[]{:S(2)}) copy-start(f32[1664]{0:T(1024)} %param.24) | copy-start | bytes 19972
  237.1 124.3 %copy-start.19 = (f32[1664]{0:T(1024)S(1)}, f32[1664]{0:T(1024)}, u32[]{:S(2)}) copy-start(f32[1664]{0:T(1024)} %param.25) | copy-start | bytes 19972
  237.1 124.3 %copy-start.38 = (f32[1664]{0:T(1024)S(1)}, f32[1664]{0:T(1024)}, u32[]{:S(2)}) copy-start(f32[1664]{0:T(1024)} %param.26) | copy-start | bytes 19972
  237.1 254.6 %all-gather.7.cloned.1.call-start = ((), (), s32[]{:S(2)}) async-start(), calls=%async_computation.6 | async-start | bytes 8785920 | tf_op jit(solution)/shard_map/all_gather | solution.py:113
  360.5 438.2 %copy-start.21 = (f32[2,257]{1,0:T(2,128)}, f32[2,257]{1,0:T(2,128)S(1)}, u32[]{:S(2)}) copy-start(f32[2,257]{1,0:T(2,128)S(1)} %broadcast_multiply_fusion.4) | copy-start | bytes 6172
  361.4 437.2 %copy-start.23 = (f32[2,257]{1,0:T(2,128)}, f32[2,257]{1,0:T(2,128)S(1)}, u32[]{:S(2)}) copy-start(f32[2,257]{1,0:T(2,128)S(1)} %add_rsqrt_fusion) | copy-start | bytes 6172
  363.6 128.1 %copy-start.39 = (f32[2048]{0:T(1024)S(1)}, f32[2048]{0:T(1024)}, u32[]{:S(2)}) copy-start(f32[2048]{0:T(1024)} %param.28) | copy-start | bytes 24580
  363.7 255.8 %all-gather.9.cloned.1.call-start = ((), (), s32[]{:S(2)}) async-start(), calls=%async_computation.8 | async-start | bytes 8785920 | tf_op jit(solution)/shard_map/all_gather | solution.py:137
  366.6 427.8 %reduce-scatter.9.cloned.1.call-start = ((), (), s32[]{:S(2)}) async-start(), calls=%async_computation.9 | async-start | bytes 8785920 | tf_op jit(solution)/shard_map/reduce_scatter | solution.py:153
  673.1 257.8 %all-gather.11.cloned.1.call-start = ((), (), s32[]{:S(2)}) async-start(), calls=%async_computation.10 | async-start | bytes 8785920 | tf_op jit(solution)/shard_map/all_gather | solution.py:168
  802.7 483.4 %all-reduce.5.cloned.1.call-start = ((), (), s32[]{:S(2)}) async-start(), calls=%async_computation.12 | async-start | bytes 38338560 | tf_op jit(solution)/shard_map/psum | solution.py:217
  802.8 68.2 %slice-start = ((s8[7028736]{0:T(1024)(128)(4,1)}), s8[4194304]{0:T(1024)(128)(4,1)S(1)}, s32[]{:S(2)}) async-start(s8[7028736]{0:T(1024)(128)(4,1)} %bitcast.176), calls=%async_computation.13 | async-start | bytes 8388608
  802.8 68.2 %slice-start.2 = ((s8[8650752]{0:T(1024)(128)(4,1)}), s8[4194304]{0:T(1024)(128)(4,1)S(1)}, s32[]{:S(2)}) async-start(s8[8650752]{0:T(1024)(128)(4,1)} %bitcast.178), calls=%async_computation.15 | async-start | bytes 8388608
  845.1 25.9 %copy-start.9 = (bf16[8,257,2048]{2,1,0:T(8,128)(2,1)}, bf16[8,257,2048]{2,1,0:T(8,128)(2,1)S(1)}, u32[]{:S(2)}) copy-start(bf16[8,257,2048]{2,1,0:T(8,128)(2,1)S(1)} %fusion.52) | copy-start | bytes 25264132
  845.1 25.9 %slice-start.1 = ((s8[7028736]{0:T(1024)(128)(4,1)}), s8[2834432]{0:T(1024)(128)(4,1)S(1)}, s32[]{:S(2)}) async-start(s8[7028736]{0:T(1024)(128)(4,1)} %bitcast.176), calls=%async_computation.14 | async-start | bytes 5668864
  1042.0 369.3 %reduce-scatter.11.cloned.1.call-start = ((), (), s32[]{:S(2)}) async-start(), calls=%async_computation.11 | async-start | bytes 8785920 | tf_op jit(solution)/shard_map/reduce_scatter | solution.py:196
  1057.4 479.8 %reduce-scatter.7.cloned.1.call-start = ((), (), s32[]{:S(2)}) async-start(), calls=%async_computation.7 | async-start | bytes 8785920 | tf_op jit(solution)/shard_map/reduce_scatter | solution.py:127
  1306.6 104.7 %copy-start.3 = (bf16[2,257,1664]{2,0,1:T(2,128)(2,1)S(1)}, bf16[2,257,1664]{2,0,1:T(2,128)(2,1)}, u32[]{:S(2)}) copy-start(bf16[2,257,1664]{2,0,1:T(2,128)(2,1)} %param.18) | copy-start | bytes 5131780
  1306.6 104.7 %copy-start.26 = (f32[2,257]{1,0:T(2,128)S(1)}, f32[2,257]{1,0:T(2,128)}, u32[]{:S(2)}) copy-start(f32[2,257]{1,0:T(2,128)} %copy-done.25) | copy-start | bytes 6172
  1306.6 104.7 %copy-start.27 = (f32[1664]{0:T(1024)S(1)}, f32[1664]{0:T(1024)}, u32[]{:S(2)}) copy-start(f32[1664]{0:T(1024)} %param.19) | copy-start | bytes 19972
  1306.6 104.7 %copy-start.29 = (f32[2,257]{1,0:T(2,128)S(1)}, f32[2,257]{1,0:T(2,128)}, u32[]{:S(2)}) copy-start(f32[2,257]{1,0:T(2,128)} %copy-done.28) | copy-start | bytes 6172
  1306.6 230.6 %copy-start.18 = (f32[1664]{0:T(1024)S(1)}, f32[1664]{0:T(1024)}, u32[]{:S(2)}) copy-start(f32[1664]{0:T(1024)} %param.24) | copy-start | bytes 19972
  1306.7 230.6 %copy-start.20 = (f32[1664]{0:T(1024)S(1)}, f32[1664]{0:T(1024)}, u32[]{:S(2)}) copy-start(f32[1664]{0:T(1024)} %param.25) | copy-start | bytes 19972
  1306.7 230.5 %copy-start.22 = (f32[2,257]{1,0:T(2,128)S(1)}, f32[2,257]{1,0:T(2,128)}, u32[]{:S(2)}) copy-start(f32[2,257]{1,0:T(2,128)} %copy-done.21) | copy-start | bytes 6172
  1306.7 230.5 %copy-start.24 = (f32[2,257]{1,0:T(2,128)S(1)}, f32[2,257]{1,0:T(2,128)}, u32[]{:S(2)}) copy-start(f32[2,257]{1,0:T(2,128)} %copy-done.23) | copy-start | bytes 6172
  1306.7 230.5 %copy-start.35 = (f32[2,257]{1,0:T(2,128)S(1)}, f32[2,257]{1,0:T(2,128)}, u32[]{:S(2)}) copy-start(f32[2,257]{1,0:T(2,128)} %copy-done.34) | copy-start | bytes 6172
  1306.7 230.5 %copy-start.37 = (f32[2,257]{1,0:T(2,128)S(1)}, f32[2,257]{1,0:T(2,128)}, u32[]{:S(2)}) copy-start(f32[2,257]{1,0:T(2,128)} %copy-done.36) | copy-start | bytes 6172
  1306.7 230.5 %copy-start.40 = (f32[1664]{0:T(1024)S(1)}, f32[1664]{0:T(1024)}, u32[]{:S(2)}) copy-start(f32[1664]{0:T(1024)} %param.30) | copy-start | bytes 19972
  1537.3 53.7 %copy-start.1 = (bf16[416,1664]{1,0:T(8,128)(2,1)S(1)}, bf16[416,1664]{1,0:T(8,128)(2,1)}, u32[]{:S(2)}) copy-start(bf16[416,1664]{1,0:T(8,128)(2,1)} %param.23) | copy-start | bytes 4153348
  (26 other events, 155.5 us)
Sparse Core Ops, SparseCore 0:
  14.6 130.0 all-gather.4
  237.2 121.0 reduce-scatter.4
  363.8 127.9 all-gather.6
  493.8 125.6 all-gather.8
  673.2 121.0 reduce-scatter.8
  802.9 127.9 all-gather.10
  1042.1 243.9 all-reduce.4
  1288.4 122.8 reduce-scatter.10
  1413.8 123.3 reduce-scatter.6
where the time goes:
time: 1610 us; the launch traced here: 1600 us
  waiting for transfers between devices  1050 us (65%)
  matrix products  270 us (17%)
  other arithmetic  112 us (7%)
  local copies, waits for them, and re-layouts  93.3 us (6%)
  blocking collectives  57.6 us (4%)
    psum x1, waiting for transfers between devices, on_device(): lax.psum(grad_qkv_weight.astype(jnp.bfloat16), 'dp').astype(jnp.float32)  186 us
    all_gather x1, waiting for transfers between devices, on_device(): normed_first = lax.all_gather(normed_local, 'tensor', axis=0, tiled=True)  130 us
    all_gather x1, waiting for transfers between devices, on_device(): lax.all_gather((unit_second * second_gain + second_shift).astype(jnp.bflo...  125 us
    reduce_scatter x1, waiting for transfers between devices, on_device(): lax.psum_scatter(jnp.einsum('isf,fd->isd', piece, down_weight, preferred_...  123 us
    reduce_scatter x1, waiting for transfers between devices, on_device(): lax.psum_scatter(jnp.einsum('isc,cd->isd', piece, out_weight, preferred_e...  121 us
    reduce_scatter x1, waiting for transfers between devices, on_device(): lax.psum_scatter(jnp.einsum('isf,df->isd', piece, up_weight, preferred_el...  121 us
    reduce_scatter x1, waiting for transfers between devices, on_device(): lax.psum_scatter(jnp.einsum('nisc,ndc->isd', piece, qkv_weight, preferred...  103 us
    all_gather x1, waiting for transfers between devices, on_device(): seed_rows = lax.all_gather(cotangent, 'tensor', axis=0, tiled=True)  99.3 us
  transfers between devices with their start and end apart: 9, of which 9 were waited for; matrix products, arithmetic and copies ran while one was open for 12% of the time, Pallas kernels for 0%

commit v1 on v0

--- a/solution.py
+++ b/solution.py
@@ -2,6 +2,7 @@
 import jax.numpy as jnp
 from jax import lax
 from jax.sharding import PartitionSpec as P
+from jax.lax import psum
 
 HD = 104
 epsilon = 1e-06
@@ -228,16 +229,19 @@
         grad_second_gain,
         grad_second_shift,
         grad_down_bias,
-    ) = lax.psum(
-        (
-            grad_first_gain,
-            grad_first_shift,
-            grad_out_bias,
-            grad_second_gain,
-            grad_second_shift,
-            grad_down_bias,
-        ),
-        ("dp", "tensor"),
+    ) = psum(
+        psum(
+            (
+                grad_first_gain,
+                grad_first_shift,
+                grad_out_bias,
+                grad_second_gain,
+                grad_second_shift,
+                grad_down_bias,
+            ),
+            axis_name="tensor",
+        ),
+        axis_name="dp",
     )
     return (
         result,

time: 1610 us -> 1610 us (level)
    psum x1 -> x2, blocking collectives: 42.1 us -> 42.2 us  [the longest x1 23.5 us: on_device(): psum(psum((grad_first_gain, grad_first_shift, grad_out_bias, grad_second_...]
where the time goes in v1:
time: 1610 us; the launch traced here: 1600 us
  waiting for transfers between devices  1050 us (65%)
  matrix products  270 us (17%)
  other arithmetic  112 us (7%)
  local copies, waits for them, and re-layouts  93.3 us (6%)
  blocking collectives  57.7 us (4%)
    psum x1, waiting for transfers between devices, on_device(): lax.psum(grad_qkv_weight.astype(jnp.bfloat16), 'dp').astype(jnp.float32)  186 us
    all_gather x1, waiting for transfers between devices, on_device(): normed_first = lax.all_gather(normed_local, 'tensor', axis=0, tiled=True)  130 us
    all_gather x1, waiting for transfers between devices, on_device(): lax.all_gather((unit_second * second_gain + second_shift).astype(jnp.bflo...  125 us
    reduce_scatter x1, waiting for transfers between devices, on_device(): lax.psum_scatter(jnp.einsum('isf,fd->isd', piece, down_weight, preferred_...  123 us
    reduce_scatter x1, waiting for transfers between devices, on_device(): lax.psum_scatter(jnp.einsum('isc,cd->isd', piece, out_weight, preferred_e...  121 us
    reduce_scatter x1, waiting for transfers between devices, on_device(): lax.psum_scatter(jnp.einsum('isf,df->isd', piece, up_weight, preferred_el...  121 us
    reduce_scatter x1, waiting for transfers between devices, on_device(): lax.psum_scatter(jnp.einsum('nisc,ndc->isd', piece, qkv_weight, preferred...  103 us
    all_gather x1, waiting for transfers between devices, on_device(): seed_rows = lax.all_gather(cotangent, 'tensor', axis=0, tiled=True)  99.3 us
  transfers between devices with their start and end apart: 9, of which 9 were waited for; matrix products, arithmetic and copies ran while one was open for 12% of the time, Pallas kernels for 0%

profile of v1, /device:TPU:0, one launch (start us, length us, event | category | flops | bytes accessed | tf_op | source)
XLA Modules:
  0.0 1597.8 jit_solution(7733901305608278045)
XLA Ops:
  14.7 130.0 %all-gather.5.cloned.1.call-done = bf16[8,257,1664]{2,1,0:T(8,128)(2,1)} async-done(((bf16[2,257,1664]{2,1,0:T(8,128)(2,1)}), bf16[8,257,1664]{2,1,0:T(8,128)(2,1)}) %all-gather.5.cloned.1.call-update) | async-done | bytes 6842384 | tf_op jit(solution)/shard_map/all_gather | solution.py:86
  144.7 15.5 convolution_bitcast_fusion
  166.4 5.9 reshape.134
  177.4 5.9 reshape.135
  196.2 24.4 %while.26 = (s32[]{:T(128)}, bf16[4,2,257,4,104]{4,2,3,1,0:T(8,128)(2,1)}, f32[4,2,4,257]{3,2,1,0:T(4,128)}, bf16[4,2,257,4,104]{4,2,3,1,0:T(8,128)(2,1)}, bf16[...) while((s32[]{:T(128)}, bf16[4,2,257,4,104]{4,2,3,1,0:T(8,128)(2,1)}, ...), condition=%wide.region_5.6_spmd, body=%wide.region_2.5_spmd.sunk | while | flops 224564544 | bytes 9116557 | solution.py:98
  228.9 8.1 convolution_convert_fusion
  237.1 121.2 %reduce-scatter.5.cloned.1.call-done = bf16[2,257,1664]{2,1,0:T(8,128)(2,1)} async-done(((bf16[8,257,1664]{2,1,0:T(8,128)(2,1)}), bf16[2,257,1664]{2,1,0:T(8,128)(2,1)}) %reduce-scatter.5.cloned.1.call-update) | async-done | bytes 1710608 | tf_op jit(solution)/shard_map/reduce_scatter | solution.py:104
  366.6 125.1 %all-gather.7.cloned.1.call-done = bf16[8,257,1664]{2,1,0:T(8,128)(2,1)} async-done(((bf16[2,257,1664]{2,1,0:T(8,128)(2,1)}), bf16[8,257,1664]{2,1,0:T(8,128)(2,1)}) %all-gather.7.cloned.1.call-update) | async-done | bytes 6842384 | tf_op jit(solution)/shard_map/all_gather | solution.py:114
  491.7 28.5 %fusion.91 = (u8[257,2048]{1,0:T(8,128)(4,1)}, u8[257,2048]{1,0:T(8,128)(4,1)}, f32[8,257,2048]{2,1,0:T(8,128)}) fusion(f32[2048]{0:T(1024)S(1)} %copy-done.39, bf16[8,257,1664]{2,1,0:T(8,128)(2,1)} %all-gather.7.cloned.1.call-done, bf16[1664,2048]{1,0:T(8,128)(2,1)} %param.27), kind=kOutput, calls=%fused_computation.123 | convolution fusion | flops 14071066624 | bytes 31561728 | tf_op jit(solution)/shard_map/isd,df->isf/dot_general | solution.py:121
  520.2 99.3 %all-gather.9.cloned.1.call-done = bf16[8,257,1664]{2,1,0:T(8,128)(2,1)} async-done(((bf16[2,257,1664]{2,1,0:T(8,128)(2,1)}), bf16[8,257,1664]{2,1,0:T(8,128)(2,1)}) %all-gather.9.cloned.1.call-update) | async-done | bytes 6842384 | tf_op jit(solution)/shard_map/all_gather | solution.py:138
  619.5 29.1 %fusion.123 = (bf16[2048]{0:T(1024)(128)(2,1)}, bf16[8,257,2048]{2,1,0:T(8,128)(2,1)S(1)}) fusion(f32[8,257,2048]{2,1,0:T(8,128)} %get-tuple-element.259, f32[2048]{0:T(1024)S(1)} %copy-done.39, bf16[8,257,1664]{2,1,0:T(8,128)(2,1)} %all-gather.9.cloned.1.call-done, bf16[2048,1664]{1,0:T(8,128)(2,1)} %param.29), kind=kOutput, calls=%fused_computation.175 | convolution fusion | flops 14063695872 | bytes 38934528 | tf_op jit(solution)/shard_map/isd,fd->isf/dot_general | solution.py:143
  652.0 21.0 %fusion.78 = bf16[8,257,1664]{2,1,0:T(8,128)(2,1)} fusion(bf16[8,257,2048]{2,1,0:T(8,128)(2,1)S(1)} %get-tuple-element.261, bf16[1664,2048]{1,0:T(8,128)(2,1)} %param.27), kind=kOutput, calls=%fused_computation.102 | convolution fusion | flops 14016590848 | bytes 22079488 | tf_op jit(solution)/shard_map/isf,df->isd/dot_general | solution.py:155
  673.1 121.2 %reduce-scatter.9.cloned.1.call-done = bf16[2,257,1664]{2,1,0:T(8,128)(2,1)} async-done(((bf16[8,257,1664]{2,1,0:T(8,128)(2,1)}), bf16[2,257,1664]{2,1,0:T(8,128)(2,1)}) %reduce-scatter.9.cloned.1.call-update) | async-done | bytes 1710608 | tf_op jit(solution)/shard_map/reduce_scatter | solution.py:154
  802.9 42.3 %fusion.52 = bf16[8,257,2048]{2,1,0:T(8,128)(2,1)S(1)} fusion(f32[8,257,2048]{2,1,0:T(8,128)} %get-tuple-element.259, f32[2048]{0:T(1024)S(1)} %copy-done.39, u8[257,2048]{1,0:T(8,128)(4,1)} %get-tuple-element.189, u8[257,2048]{1,0:T(8,128)(4,1)} %get-tuple-element.188), kind=kLoop, calls=%fused_computation.60 | loop fusion | flops 298958848 | bytes 26324992 | tf_op jit(solution)/shard_map/convert_element_type | solution.py:124
  845.2 25.8 %bitcast_convert_fusion.1 = bf16[2048,1664]{1,0:T(8,128)(2,1)} fusion(bf16[8,257,2048]{2,1,0:T(8,128)(2,1)S(1)} %fusion.52, bf16[8,257,1664]{2,1,0:T(8,128)(2,1)} %all-gather.9.cloned.1.call-done), kind=kOutput, calls=%fused_computation.86 | convolution fusion | flops 14016577536 | bytes 22079488 | tf_op jit(solution)/shard_map/isf,isd->fd/dot_general | solution.py:139
  871.1 18.5 %bitcast_convert_fusion.2 = bf16[1664,2048]{1,0:T(8,128)(2,1)} fusion(bf16[8,257,1664]{2,1,0:T(8,128)(2,1)S(1)} %bitcast.177, bf16[8,257,2048]{2,1,0:T(8,128)(2,1)S(1)} %bitcast.179), kind=kOutput, calls=%fused_computation.87 | convolution fusion | flops 14016577536 | bytes 22079488 | tf_op jit(solution)/shard_map/isd,isf->df/dot_general | solution.py:149
  889.5 41.3 %all-gather.11.cloned.1.call-done = bf16[8,257,1664]{2,1,0:T(8,128)(2,1)} async-done(((bf16[2,257,1664]{2,1,0:T(8,128)(2,1)}), bf16[8,257,1664]{2,1,0:T(8,128)(2,1)}) %all-gather.11.cloned.1.call-update) | async-done | bytes 6842384 | tf_op jit(solution)/shard_map/all_gather | solution.py:169
  930.9 8.4 convolution_convert_fusion.1
  944.1 50.2 %while.27 = (s32[]{:T(128)}, bf16[4,2,257,4,104]{4,2,3,1,0:T(8,128)(2,1)}, bf16[4,2,257,4,104]{4,3,2,1,0:T(4,128)(2,1)}, bf16[4,2,257,4,104]{4,2,3,1,0:T(8,128)(...) while((s32[]{:T(128)}, ...), condition=%wide.region_15.16_spmd, body=%wide.region_13.15_spmd.sunk | while | flops 556935424 | bytes 23355692 | solution.py:176
  1018.4 8.0 fusion.116
  1026.4 15.7 fusion.98
  1042.1 15.3 bitcast_convert_fusion
  1057.5 21.5 %fusion.81 = bf16[8,257,1664]{2,1,0:T(8,128)(2,1)} fusion(bf16[8,257,2048]{2,1,0:T(8,128)(2,1)} %copy-done.9, bf16[2048,1664]{1,0:T(8,128)(2,1)} %param.29), kind=kOutput, calls=%fused_computation.103 | convolution fusion | flops 14016590848 | bytes 22079488 | tf_op jit(solution)/shard_map/isf,fd->isd/dot_general | solution.py:129
  1083.4 15.5 all-reduce.2
  1100.1 186.1 %all-reduce.6.cloned.1.call-done = (bf16[3,1664,416]{1,2,0:T(8,128)(2,1)}, bf16[416,1664]{1,0:T(8,128)(2,1)}, bf16[1664,2048]{1,0:T(8,128)(2,1)}, bf16[2048,1664]{1,0:T(8,128)(2,1)}) async-done(((bf16[3,1664,416]{1,2,0:T(8,128)(2,1)}, bf16[416,1664]{1,0:T(8,128)(2,1)}, bf16[1664,2048]{1,0:T(8,128)(2,1)}, bf16[2048,1664]{1,0:T(8,128)(2,1)}), (bf16[3,1664,416]{1,2,0:T(8,128)(2,1)}, ...) | async-done | bytes 19169296 | tf_op jit(solution)/shard_map/psum | solution.py:218
  1286.2 10.6 convert_element_type.181
  1296.8 6.0 convert_element_type.184
  1308.5 102.9 %reduce-scatter.11.cloned.1.call-done = bf16[2,257,1664]{2,1,0:T(8,128)(2,1)} async-done(((bf16[8,257,1664]{2,1,0:T(8,128)(2,1)}), bf16[2,257,1664]{2,1,0:T(8,128)(2,1)}) %reduce-scatter.11.cloned.1.call-update) | async-done | bytes 1710608 | tf_op jit(solution)/shard_map/reduce_scatter | solution.py:197
  1414.4 122.8 %reduce-scatter.7.cloned.1.call-done = bf16[2,257,1664]{2,1,0:T(8,128)(2,1)} async-done(((bf16[8,257,1664]{2,1,0:T(8,128)(2,1)}), bf16[2,257,1664]{2,1,0:T(8,128)(2,1)}) %reduce-scatter.7.cloned.1.call-update) | async-done | bytes 1710608 | tf_op jit(solution)/shard_map/reduce_scatter | solution.py:128
  1537.3 6.4 fusion.108
  1548.8 18.7 %all-reduce.1 = (f32[1664]{0:T(1024)S(1)}, f32[1664]{0:T(1024)S(1)}, f32[1664]{0:T(1024)S(1)}, f32[1664]{0:T(1024)S(1)}, f32[1664]{0:T(1024)S(1)}, /*index=5*/f32[1664]{0:T(1024)S(1)}) all-reduce(f32[1664]{0:T(1024)S(1)} %get-tuple-element.192, f32[1664]{0:T(1024)S(1)} %get-tuple-element.197, ...), channel_id=1, replica_groups=mesh['dp'=8,'tensor'=4] {'tensor'}, use_global_device_ids=true, to_apply=%region_20.21 | all-reduce | flops 9984 | bytes 79872 | tf_op jit(solution)/shard_map/psum | solution.py:233
  1567.5 23.5 %all-reduce = (f32[1664]{0:T(1024)}, f32[1664]{0:T(1024)}, f32[1664]{0:T(1024)}, f32[1664]{0:T(1024)}, f32[1664]{0:T(1024)}, /*index=5*/f32[1664]{0:T(1024)}) all-reduce(f32[1664]{0:T(1024)S(1)} %get-tuple-element.236, f32[1664]{0:T(1024)S(1)} %get-tuple-element.237, ...), channel_id=1, replica_groups=mesh['dp'=8,'tensor'=4] {'dp'}, use_global_device_ids=true, to_apply=%region_21.22 | all-reduce | flops 9984 | bytes 79872 | tf_op jit(solution)/shard_map/psum | solution.py:232
  (225 shorter events, 182.8 us)
Async XLA Ops:
  7.2 221.7 %copy-start = (bf16[416,1664]{1,0:T(8,128)(2,1)S(1)}, bf16[416,1664]{1,0:T(8,128)(2,1)}, u32[]{:S(2)}) copy-start(bf16[416,1664]{1,0:T(8,128)(2,1)} %param.23) | copy-start | bytes 4153348
  7.2 137.5 %all-gather.5.cloned.1.call-start = ((), (), s32[]{:S(2)}) async-start(), calls=%async_computation.4 | async-start | bytes 8785920 | tf_op jit(solution)/shard_map/all_gather | solution.py:86
  14.5 343.9 %reduce-scatter.5.cloned.1.call-start = ((), (), s32[]{:S(2)}) async-start(), calls=%async_computation.5 | async-start | bytes 8785920 | tf_op jit(solution)/shard_map/reduce_scatter | solution.py:104
  237.0 121.3 %copy-start.17 = (f32[1664]{0:T(1024)S(1)}, f32[1664]{0:T(1024)}, u32[]{:S(2)}) copy-start(f32[1664]{0:T(1024)} %param.24) | copy-start | bytes 19972
  237.1 124.4 %copy-start.19 = (f32[1664]{0:T(1024)S(1)}, f32[1664]{0:T(1024)}, u32[]{:S(2)}) copy-start(f32[1664]{0:T(1024)} %param.25) | copy-start | bytes 19972
  237.1 124.4 %copy-start.38 = (f32[1664]{0:T(1024)S(1)}, f32[1664]{0:T(1024)}, u32[]{:S(2)}) copy-start(f32[1664]{0:T(1024)} %param.26) | copy-start | bytes 19972
  237.1 254.6 %all-gather.7.cloned.1.call-start = ((), (), s32[]{:S(2)}) async-start(), calls=%async_computation.6 | async-start | bytes 8785920 | tf_op jit(solution)/shard_map/all_gather | solution.py:114
  360.5 438.2 %copy-start.21 = (f32[2,257]{1,0:T(2,128)}, f32[2,257]{1,0:T(2,128)S(1)}, u32[]{:S(2)}) copy-start(f32[2,257]{1,0:T(2,128)S(1)} %broadcast_multiply_fusion.4) | copy-start | bytes 6172
  361.5 437.2 %copy-start.23 = (f32[2,257]{1,0:T(2,128)}, f32[2,257]{1,0:T(2,128)S(1)}, u32[]{:S(2)}) copy-start(f32[2,257]{1,0:T(2,128)S(1)} %add_rsqrt_fusion) | copy-start | bytes 6172
  363.6 128.1 %copy-start.39 = (f32[2048]{0:T(1024)S(1)}, f32[2048]{0:T(1024)}, u32[]{:S(2)}) copy-start(f32[2048]{0:T(1024)} %param.28) | copy-start | bytes 24580
  363.7 255.8 %all-gather.9.cloned.1.call-start = ((), (), s32[]{:S(2)}) async-start(), calls=%async_computation.8 | async-start | bytes 8785920 | tf_op jit(solution)/shard_map/all_gather | solution.py:138
  366.6 427.7 %reduce-scatter.9.cloned.1.call-start = ((), (), s32[]{:S(2)}) async-start(), calls=%async_computation.9 | async-start | bytes 8785920 | tf_op jit(solution)/shard_map/reduce_scatter | solution.py:154
  673.1 257.8 %all-gather.11.cloned.1.call-start = ((), (), s32[]{:S(2)}) async-start(), calls=%async_computation.10 | async-start | bytes 8785920 | tf_op jit(solution)/shard_map/all_gather | solution.py:169
  802.8 483.4 %all-reduce.6.cloned.1.call-start = ((), (), s32[]{:S(2)}) async-start(), calls=%async_computation.12 | async-start | bytes 38338560 | tf_op jit(solution)/shard_map/psum | solution.py:218
  802.8 68.2 %slice-start = ((s8[7028736]{0:T(1024)(128)(4,1)}), s8[4194304]{0:T(1024)(128)(4,1)S(1)}, s32[]{:S(2)}) async-start(s8[7028736]{0:T(1024)(128)(4,1)} %bitcast.176), calls=%async_computation.13 | async-start | bytes 8388608
  802.8 68.2 %slice-start.2 = ((s8[8650752]{0:T(1024)(128)(4,1)}), s8[4194304]{0:T(1024)(128)(4,1)S(1)}, s32[]{:S(2)}) async-start(s8[8650752]{0:T(1024)(128)(4,1)} %bitcast.178), calls=%async_computation.15 | async-start | bytes 8388608
  845.2 25.9 %copy-start.9 = (bf16[8,257,2048]{2,1,0:T(8,128)(2,1)}, bf16[8,257,2048]{2,1,0:T(8,128)(2,1)S(1)}, u32[]{:S(2)}) copy-start(bf16[8,257,2048]{2,1,0:T(8,128)(2,1)S(1)} %fusion.52) | copy-start | bytes 25264132
  845.2 25.9 %slice-start.1 = ((s8[7028736]{0:T(1024)(128)(4,1)}), s8[2834432]{0:T(1024)(128)(4,1)S(1)}, s32[]{:S(2)}) async-start(s8[7028736]{0:T(1024)(128)(4,1)} %bitcast.176), calls=%async_computation.14 | async-start | bytes 5668864
  1042.1 369.3 %reduce-scatter.11.cloned.1.call-start = ((), (), s32[]{:S(2)}) async-start(), calls=%async_computation.11 | async-start | bytes 8785920 | tf_op jit(solution)/shard_map/reduce_scatter | solution.py:197
  1057.5 479.8 %reduce-scatter.7.cloned.1.call-start = ((), (), s32[]{:S(2)}) async-start(), calls=%async_computation.7 | async-start | bytes 8785920 | tf_op jit(solution)/shard_map/reduce_scatter | solution.py:128
  1306.7 104.7 %copy-start.3 = (bf16[2,257,1664]{2,0,1:T(2,128)(2,1)S(1)}, bf16[2,257,1664]{2,0,1:T(2,128)(2,1)}, u32[]{:S(2)}) copy-start(bf16[2,257,1664]{2,0,1:T(2,128)(2,1)} %param.18) | copy-start | bytes 5131780
  1306.7 104.7 %copy-start.26 = (f32[2,257]{1,0:T(2,128)S(1)}, f32[2,257]{1,0:T(2,128)}, u32[]{:S(2)}) copy-start(f32[2,257]{1,0:T(2,128)} %copy-done.25) | copy-start | bytes 6172
  1306.7 104.7 %copy-start.27 = (f32[1664]{0:T(1024)S(1)}, f32[1664]{0:T(1024)}, u32[]{:S(2)}) copy-start(f32[1664]{0:T(1024)} %param.19) | copy-start | bytes 19972
  1306.7 104.7 %copy-start.29 = (f32[2,257]{1,0:T(2,128)S(1)}, f32[2,257]{1,0:T(2,128)}, u32[]{:S(2)}) copy-start(f32[2,257]{1,0:T(2,128)} %copy-done.28) | copy-start | bytes 6172
  1306.7 230.6 %copy-start.18 = (f32[1664]{0:T(1024)S(1)}, f32[1664]{0:T(1024)}, u32[]{:S(2)}) copy-start(f32[1664]{0:T(1024)} %param.24) | copy-start | bytes 19972
  1306.7 230.6 %copy-start.20 = (f32[1664]{0:T(1024)S(1)}, f32[1664]{0:T(1024)}, u32[]{:S(2)}) copy-start(f32[1664]{0:T(1024)} %param.25) | copy-start | bytes 19972
  1306.7 230.5 %copy-start.22 = (f32[2,257]{1,0:T(2,128)S(1)}, f32[2,257]{1,0:T(2,128)}, u32[]{:S(2)}) copy-start(f32[2,257]{1,0:T(2,128)} %copy-done.21) | copy-start | bytes 6172
  1306.7 230.5 %copy-start.24 = (f32[2,257]{1,0:T(2,128)S(1)}, f32[2,257]{1,0:T(2,128)}, u32[]{:S(2)}) copy-start(f32[2,257]{1,0:T(2,128)} %copy-done.23) | copy-start | bytes 6172
  1306.7 230.5 %copy-start.35 = (f32[2,257]{1,0:T(2,128)S(1)}, f32[2,257]{1,0:T(2,128)}, u32[]{:S(2)}) copy-start(f32[2,257]{1,0:T(2,128)} %copy-done.34) | copy-start | bytes 6172
  1306.7 230.5 %copy-start.37 = (f32[2,257]{1,0:T(2,128)S(1)}, f32[2,257]{1,0:T(2,128)}, u32[]{:S(2)}) copy-start(f32[2,257]{1,0:T(2,128)} %copy-done.36) | copy-start | bytes 6172
  1306.8 230.5 %copy-start.40 = (f32[1664]{0:T(1024)S(1)}, f32[1664]{0:T(1024)}, u32[]{:S(2)}) copy-start(f32[1664]{0:T(1024)} %param.30) | copy-start | bytes 19972
  1543.8 47.3 %copy-start.1 = (bf16[416,1664]{1,0:T(8,128)(2,1)S(1)}, bf16[416,1664]{1,0:T(8,128)(2,1)}, u32[]{:S(2)}) copy-start(bf16[416,1664]{1,0:T(8,128)(2,1)} %param.23) | copy-start | bytes 4153348
  (26 other events, 155.7 us)
Sparse Core Ops, SparseCore 0:
  14.6 130.0 all-gather.4
  237.2 121.1 reduce-scatter.4
  363.8 127.9 all-gather.6
  493.8 125.6 all-gather.8
  673.2 121.0 reduce-scatter.8
  802.9 127.9 all-gather.10
  1042.2 243.9 all-reduce.5
  1288.5 122.8 reduce-scatter.10
  1413.8 123.3 reduce-scatter.6
